TPU v7x, 32 devices: a whole 2x2x4 slice. The times are simulated.
32 devices in a mesh: layer: 2 (over core), latent: 8 (over z, x), token: 2 (over y).
Axes of the slice: x: 2, y: 2, z: 4, core: 2. Of those that a mesh axis runs over, the one named last changes fastest.
Arguments:
- taps: bfloat16 [2, 448, 3584], P('layer', 'token'), may hold values from -6 to 6
- token_ids: int32 [448], P('token'), may hold values from 2 to 255999, as said below
- enc_weight: bfloat16 [2, 3584, 2048], P('layer', 'token', 'latent'), may hold values from -0.0625 to 0.0625
- enc_bias: float32 [2048], P('latent'), may hold values from -3 to 3
- dec_weight: bfloat16 [2, 3584, 2048], P('layer', 'token', 'latent'), as said below
- dec_bias: float32 [2, 3584], P('layer'), may hold values from -3 to 3
Outputs:
- enc_grad: bfloat16 [2, 3584, 2048], P('layer', 'token', 'latent')
- dec_grad: bfloat16 [2, 3584, 2048], P('layer', 'token', 'latent')
Inputs may be any that keep to these rules, and one draw needn't show every extreme that they name: `token_ids`: id 2 marks the beginning of a document and stands at position 0; all other ids are 3 or more. `dec_weight`: entries of order 2048^-0.5.
All inputs are finite; a program needn't handle non-finite values.
Results may differ from a plain program's by a relative error of at most 0.014.
Values may be sent and summed in bfloat16 or wider, within the bound.
No kernel may reach another device: no remote copies, remote signals or barrier semaphores. Data moves between devices by JAX's collectives and lax.ppermute only.
A program may use at most 64 MiB of HBM per device.

v0:
```python
import math
import jax
import jax.numpy as jnp
from jax import lax
from jax.sharding import PartitionSpec as P

KNEE_WIDTH = 0.5
SPARSITY = 0.5
BEGIN_TOKEN = 2


def smooth_relu(preact):
    positive = jnp.maximum(preact, 0.0)
    return jnp.where(
        positive < KNEE_WIDTH, positive * positive / (2.0 * KNEE_WIDTH), positive - 0.5 * KNEE_WIDTH
    )


def relu_slope(preact):
    return jnp.clip(preact / KNEE_WIDTH, 0.0, 1.0)


def local(taps, token_ids, enc_weight, enc_bias, dec_weight, dec_bias):
    tap_rows = taps[0]
    tokens_dev = tap_rows.shape[0]
    latent_dev = enc_weight.shape[2]
    row_block = enc_weight.shape[1]
    loss_scale = 1.0 / math.sqrt(tokens_dev * lax.axis_size("token"))
    keep_mask = (token_ids != BEGIN_TOKEN).astype(jnp.float32)
    spread = lax.all_to_all(tap_rows, "token", split_axis=1, concat_axis=0, tiled=True)
    partial_pre = lax.psum_scatter(
        jnp.dot(spread, enc_weight[0], preferred_element_type=jnp.float32),
        "token",
        scatter_dimension=0,
        tiled=True,
    )
    preact = lax.psum(partial_pre, "layer") + enc_bias[None, :]
    features = smooth_relu(preact).astype(jnp.bfloat16)
    dec_full = lax.all_gather(dec_weight[0], "token", axis=0, tiled=True)
    rebuilt_part = lax.dot_general(
        features, dec_full, (((1,), (1,)), ((), ())), preferred_element_type=jnp.float32
    )
    rebuilt = lax.psum(rebuilt_part, "latent") + dec_bias[0][None, :]
    residue = (loss_scale * keep_mask[:, None] * (rebuilt - tap_rows.astype(jnp.float32))).astype(
        jnp.bfloat16
    )
    colnorm = jnp.sqrt(jnp.sum(jnp.square(dec_full.astype(jnp.float32)), axis=0) + 1e-06)
    back_part = jnp.dot(residue, dec_full, preferred_element_type=jnp.float32)
    feat_back, norm_total = lax.psum((back_part, colnorm), "layer")
    feat_grads = feat_back + loss_scale * SPARSITY * keep_mask[:, None] * norm_total[None, :]
    pre_grads = (feat_grads * relu_slope(preact)).astype(jnp.bfloat16)
    activity = jnp.sum(keep_mask[:, None] * features.astype(jnp.float32), axis=0)
    penalty_scale = loss_scale * SPARSITY * activity / colnorm
    product = lax.dot_general(
        residue, features, (((0,), (0,)), ((), ())), preferred_element_type=jnp.float32
    )
    dec_grad = lax.psum_scatter(
        (product + dec_full.astype(jnp.float32) * penalty_scale[None, :]).astype(jnp.bfloat16),
        "token",
        scatter_dimension=0,
        tiled=True,
    )
    code_rows = lax.all_gather(pre_grads, "token", axis=0, tiled=True)
    blocks = lax.axis_size("token")
    spread_blocks = spread.reshape(blocks, tokens_dev, row_block)
    code_blocks = code_rows.reshape(blocks, tokens_dev, latent_dev)
    block_terms = jnp.einsum(
        "btd,btk->bdk", spread_blocks, code_blocks, preferred_element_type=jnp.float32
    )
    enc_grad = jnp.sum(
        lax.optimization_barrier(block_terms.astype(jnp.bfloat16)).astype(jnp.float32), axis=0
    )
    return (enc_grad.astype(jnp.bfloat16)[None], dec_grad[None])


def solution(mesh):
    placed = (
        P("layer", "token", None),
        P("token"),
        P("layer", "token", "latent"),
        P("latent"),
        P("layer", "token", "latent"),
        P("layer", None),
    )
    return jax.shard_map(
        local,
        mesh=mesh,
        in_specs=placed,
        out_specs=(P("layer", "token", "latent"), P("layer", "token", "latent")),
        check_vma=False,
    )
```

profile of v0, /device:TPU:0, one launch (start us, length us, event | category | flops | bytes accessed | tf_op | source)
XLA Modules:
  0.0 302.7 jit_solution(5209254433351047432)
XLA Ops:
  7.2 3.7 %all_to_all.14 = bf16[224,2,1792]{2,1,0:T(2,128)(2,1)S(1)} reshape(bf16[1,224,3584]{2,1,0:T(8,128)(2,1)} %param.6) | data formatting | bytes 3211264 | tf_op jit(solution)/shard_map/all_to_all | solution.py:30
  11.1 23.6 %all_to_all.19 = bf16[224,2,1792]{2,0,1:T(8,128)(2,1)S(1)} all-to-all(bf16[224,2,1792]{2,0,1:T(8,128)(2,1)S(1)} %copy.9), channel_id=1, replica_groups=mesh['layer'=2,'latent'=8,'token'=2] {'token'}, dimensions={1} | all-to-all | bytes 3211264 | tf_op jit(solution)/shard_map/all_to_all | solution.py:30
  34.7 1.3 copy-done.3
  36.0 1.4 fusion.10
  37.4 14.5 %reduce-scatter.3.cloned.1.call-done = f32[224,256]{1,0:T(8,128)} async-done(((f32[448,256]{1,0:T(8,128)}), f32[224,256]{1,0:T(8,128)}) %reduce-scatter.3.cloned.1.call-update) | async-done | bytes 229392 | tf_op jit(solution)/shard_map/reduce_scatter | solution.py:31
  52.0 0.7 all-gather.3.cloned.1.call-update
  52.8 19.7 %all-reduce.4.cloned.1.call-done = f32[224,256]{1,0:T(8,128)} async-done(((f32[224,256]{1,0:T(8,128)}), f32[224,256]{1,0:T(8,128)}) %all-reduce.4.cloned.1.call-update) | async-done | bytes 229392 | tf_op jit(solution)/shard_map/psum | solution.py:37
  72.4 1.1 multiply_reduce_fusion
  73.5 31.9 %all-gather.3.cloned.1.call-done = bf16[1,3584,256]{2,1,0:T(8,128)(2,1)} async-done(((bf16[1,1792,256]{2,1,0:T(8,128)(2,1)}), bf16[1,3584,256]{2,1,0:T(8,128)(2,1)}) %all-gather.3.cloned.1.call-update) | async-done | bytes 1835024 | tf_op jit(solution)/shard_map/all_gather | solution.py:39
  105.4 3.9 %fusion.7 = f32[224,3584]{1,0:T(8,128)} fusion(bf16[224,256]{1,0:T(8,128)(2,1)S(1)} %get-tuple-element.5, bf16[1,3584,256]{2,1,0:T(8,128)(2,1)} %all-gather.3.cloned.1.call-done), kind=kOutput, calls=%fused_computation.12 | convolution fusion | flops 411041792 | bytes 5160960 | tf_op jit(solution)/shard_map/dot_general | solution.py:40
  110.1 0.8 copy-done.1
  111.3 129.0 %all-reduce.6.cloned.1.call-done = f32[224,3584]{1,0:T(8,128)} async-done(((f32[224,3584]{1,0:T(8,128)}), f32[224,3584]{1,0:T(8,128)}) %all-reduce.6.cloned.1.call-update) | async-done | bytes 3211280 | tf_op jit(solution)/shard_map/psum | solution.py:43
  240.3 2.9 fusion.3
  243.2 1.1 copy-done.2
  244.3 1.3 fusion.5
  245.7 3.4 %fusion = bf16[3584,256]{1,0:T(8,128)(2,1)} fusion(bf16[224,3584]{1,0:T(8,128)(2,1)} %copy-done.2, bf16[224,256]{1,0:T(8,128)(2,1)S(1)} %get-tuple-element.5, bf16[1,3584,256]{2,1,0:T(8,128)(2,1)S(1)} %copy-done.1, f32[256]{0:T(256)S(1)} %get-tuple-element.6), kind=kOutput, calls=%fused_computation.1 | convolution fusion | flops 414711808 | bytes 5391360 | tf_op jit(solution)/shard_map/dot_general | solution.py:54
  249.1 2.6 psum.31
  251.7 11.2 %all-reduce.8.cloned.1.call-done = f32[224,256]{1,0:T(8,128)} async-done(((f32[224,256]{1,0:T(8,128)}), f32[224,256]{1,0:T(8,128)}) %all-reduce.8.cloned.1.call-update) | async-done | bytes 229392 | tf_op jit(solution)/shard_map/psum | solution.py:49
  262.9 1.0 multiply_convert_fusion
  264.0 6.0 %all_gather.7 = bf16[448,256]{1,0:T(8,128)(2,1)S(1)} all-gather(bf16[224,256]{1,0:T(8,128)(2,1)S(1)} %multiply_convert_fusion), channel_id=1, replica_groups=mesh['layer'=2,'latent'=8,'token'=2] {'token'}, dimensions={0}, use_global_device_ids=true | all-gather | bytes 344064 | tf_op jit(solution)/shard_map/all_gather | solution.py:63
  270.0 2.1 fusion.4
  272.1 1.5 reduce_sum.31
  273.6 2.2 copy.10
  275.8 20.1 %reduce-scatter.5.cloned.1.call-done = bf16[1792,256]{1,0:T(8,128)(2,1)} async-done(((bf16[3584,256]{1,0:T(8,128)(2,1)}), bf16[1792,256]{1,0:T(8,128)(2,1)}) %reduce-scatter.5.cloned.1.call-update) | async-done | bytes 917520 | tf_op jit(solution)/shard_map/reduce_scatter | solution.py:57
  (30 shorter events, 1.7 us)
Async XLA Ops:
  7.2 28.9 %copy-start = (bf16[1,1792,256]{2,1,0:T(8,128)(2,1)S(1)}, bf16[1,1792,256]{2,1,0:T(8,128)(2,1)}, u32[]{:S(2)}) copy-start(bf16[1,1792,256]{2,1,0:T(8,128)(2,1)} %param.8) | copy-start | bytes 2752516
  7.2 44.8 %reduce-scatter.3.cloned.1.call-start = ((), (), s32[]{:S(2)}) async-start(), calls=%async_computation.3 | async-start | bytes 688128 | tf_op jit(solution)/shard_map/reduce_scatter | solution.py:31
  34.7 1.3 copy-start.3
  36.0 16.7 %copy-start.7 = (s32[224]{0:T(256)S(1)}, s32[224]{0:T(256)}, u32[]{:S(2)}) copy-start(s32[224]{0:T(256)} %param.7) | copy-start | bytes 2692
  36.0 36.4 %copy-start.6 = (f32[256]{0:T(256)S(1)}, f32[256]{0:T(256)}, u32[]{:S(2)}) copy-start(f32[256]{0:T(256)} %param.9) | copy-start | bytes 3076
  37.4 35.0 %all-reduce.4.cloned.1.call-start = ((), (), s32[]{:S(2)}) async-start(), calls=%async_computation.4 | async-start | bytes 458752 | tf_op jit(solution)/shard_map/psum | solution.py:37
  52.0 53.4 %all-gather.3.cloned.1.call-start = ((), (), s32[]{:S(2)}) async-start(), calls=%async_computation.8 | async-start | bytes 2752512 | tf_op jit(solution)/shard_map/all_gather | solution.py:39
  52.7 187.6 %all-reduce.6.cloned.1.call-start = ((), (), s32[]{:S(2)}) async-start(), calls=%async_computation.5 | async-start | bytes 6422528 | tf_op jit(solution)/shard_map/psum | solution.py:43
  109.3 0.7 copy-start.5
  109.3 1.5 copy-start.1
  109.3 153.6 %all-reduce.8.cloned.1.call-start = ((), (), s32[]{:S(2)}) async-start(), calls=%async_computation.6 | async-start | bytes 458752 | tf_op jit(solution)/shard_map/psum | solution.py:49
  243.2 1.2 copy-start.2
  245.6 50.3 %reduce-scatter.5.cloned.1.call-start = ((), (), s32[]{:S(2)}) async-start(), calls=%async_computation.7 | async-start | bytes 2752512 | tf_op jit(solution)/shard_map/reduce_scatter | solution.py:57
  249.1 13.9 %copy-start.4 = (f32[224,256]{1,0:T(8,128)S(1)}, f32[224,256]{1,0:T(8,128)}, u32[]{:S(2)}) copy-start(f32[224,256]{1,0:T(8,128)} %all-reduce.4.cloned.1.call-done) | copy-start | bytes 688132
Sparse Core Ops, SparseCore 0:
  37.5 14.3 reduce-scatter.2
  54.3 18.1 all-reduce.3
  74.0 31.3 all-gather.2
  109.5 130.8 all-reduce.5
  245.8 17.1 all-reduce.7
  265.6 30.2 reduce-scatter.4
where the time goes:
time: 303 us
  waiting for transfers between devices  227 us (75%)
  blocking collectives  32.2 us (11%)
  between operations  14.2 us (5%)
  matrix products  12 us (4%)
  local copies, waits for them, and re-layouts  9.91 us (3%)
  other arithmetic  7.02 us (2%)
    psum x1, waiting for transfers between devices, local(): rebuilt = lax.psum(rebuilt_part, 'latent') + dec_bias[0][None, :]  129 us
    all_gather x1, waiting for transfers between devices, local(): dec_full = lax.all_gather(dec_weight[0], 'token', axis=0, tiled=True)  31.9 us
    all_to_all x1, blocking collectives, local(): lax.all_to_all(tap_rows, 'token', split_axis=1, concat_axis=0, tiled=True)  23.6 us
    reduce_scatter x1, waiting for transfers between devices, local(): lax.psum_scatter((product + dec_full.astype(jnp.float32) * penalty_scale[...  20.1 us
    psum x1, waiting for transfers between devices, local(): preact = lax.psum(partial_pre, 'layer') + enc_bias[None, :]  19.7 us
    reduce_scatter x1, waiting for transfers between devices, local(): lax.psum_scatter(jnp.dot(spread, enc_weight[0], preferred_element_type=jn...  14.5 us
    psum x1, waiting for transfers between devices, local(): feat_back, norm_total = lax.psum((back_part, colnorm), 'layer')  11.2 us
  transfers between devices with their start and end apart: 6, of which 6 were waited for; matrix products, arithmetic and copies ran while one was open for 4% of the time, Pallas kernels for 0%

commit v1 on v0

--- a/solution.py
+++ b/solution.py
@@ -40,7 +40,7 @@
     rebuilt_part = lax.dot_general(
         features, dec_full, (((1,), (1,)), ((), ())), preferred_element_type=jnp.float32
     )
-    rebuilt = lax.psum(rebuilt_part, "latent") + dec_bias[0][None, :]
+    rebuilt = jnp.sum(lax.all_gather(rebuilt_part, "latent"), axis=0) + dec_bias[0][None, :]
     residue = (loss_scale * keep_mask[:, None] * (rebuilt - tap_rows.astype(jnp.float32))).astype(
         jnp.bfloat16
     )

time: 303 us -> 675 us (2.23)
  waiting for transfers between devices: 227 us -> 587 us
  other arithmetic: 7.02 us -> 18.6 us
    all_gather x0 -> x1, waiting for transfers between devices: none -> 488 us  [local(): lax.all_gather(rebuilt_part, 'latent')]
    psum x1 -> x0, waiting for transfers between devices: 129 us -> none  [local(): rebuilt = lax.psum(rebuilt_part, 'latent') + dec_bias[0][None, :]]
    reduce_sum x0 -> x1, other arithmetic: none -> 11.5 us  [local(): jnp.sum(lax.all_gather(rebuilt_part, 'latent'), axis=0)]
  transfers between devices with their start and end apart: 6 -> 6, of which waited for: 6 -> 6; matrix products, arithmetic and copies ran while one was open for 4% -> 2% of each run, Pallas kernels for 0% -> 0%
where the time goes in v1:
time: 675 us; the launch traced here: 674 us
  waiting for transfers between devices  587 us (87%)
  blocking collectives  32.2 us (5%)
  other arithmetic  18.6 us (3%)
  between operations  14.2 us (2%)
  matrix products  12 us (2%)
  local copies, waits for them, and re-layouts  9.8 us (1%)
    all_gather x1, waiting for transfers between devices, local(): lax.all_gather(rebuilt_part, 'latent')  488 us
    all_gather x1, waiting for transfers between devices, local(): dec_full = lax.all_gather(dec_weight[0], 'token', axis=0, tiled=True)  31.9 us
    all_to_all x1, blocking collectives, local(): lax.all_to_all(tap_rows, 'token', split_axis=1, concat_axis=0, tiled=True)  23.6 us
    reduce_scatter x1, waiting for transfers between devices, local(): lax.psum_scatter((product + dec_full.astype(jnp.float32) * penalty_scale[...  20.1 us
    psum x1, waiting for transfers between devices, local(): preact = lax.psum(partial_pre, 'layer') + enc_bias[None, :]  19.7 us
    reduce_scatter x1, waiting for transfers between devices, local(): lax.psum_scatter(jnp.dot(spread, enc_weight[0], preferred_element_type=jn...  14.5 us
  transfers between devices with their start and end apart: 6, of which 6 were waited for; matrix products, arithmetic and copies ran while one was open for 2% of the time, Pallas kernels for 0%

profile of v1, /device:TPU:0, one launch (start us, length us, event | category | flops | bytes accessed | tf_op | source)
XLA Modules:
  0.0 674.5 jit_solution(6176081308186872619)
XLA Ops:
  7.2 3.7 all_to_all.14
  11.1 23.6 %all_to_all.19 = bf16[224,2,1792]{2,0,1:T(8,128)(2,1)S(1)} all-to-all(bf16[224,2,1792]{2,0,1:T(8,128)(2,1)S(1)} %copy.9), channel_id=1, replica_groups=mesh['layer'=2,'latent'=8,'token'=2] {'token'}, dimensions={1} | all-to-all | bytes 3211264 | tf_op jit(solution)/shard_map/all_to_all | solution.py:30
  34.7 1.2 copy-done.3
  35.9 1.4 fusion.10
  37.3 14.5 %reduce-scatter.3.cloned.1.call-done = f32[224,256]{1,0:T(8,128)} async-done(((f32[448,256]{1,0:T(8,128)}), f32[224,256]{1,0:T(8,128)}) %reduce-scatter.3.cloned.1.call-update) | async-done | bytes 229392 | tf_op jit(solution)/shard_map/reduce_scatter | solution.py:31
  52.7 19.7 %all-reduce.3.cloned.1.call-done = f32[224,256]{1,0:T(8,128)} async-done(((f32[224,256]{1,0:T(8,128)}), f32[224,256]{1,0:T(8,128)}) %all-reduce.3.cloned.1.call-update) | async-done | bytes 229392 | tf_op jit(solution)/shard_map/psum | solution.py:37
  72.3 1.1 multiply_reduce_fusion
  73.4 31.9 %all-gather.5.cloned.1.call-done = bf16[1,3584,256]{2,1,0:T(8,128)(2,1)} async-done(((bf16[1,1792,256]{2,1,0:T(8,128)(2,1)}), bf16[1,3584,256]{2,1,0:T(8,128)(2,1)}) %all-gather.5.cloned.1.call-update) | async-done | bytes 1835024 | tf_op jit(solution)/shard_map/all_gather | solution.py:39
  105.3 3.9 fusion.7
  109.9 0.8 copy-done.1
  111.2 488.3 %all-gather.7.cloned.1.call-done = f32[1792,3584]{1,0:T(8,128)} async-done(((f32[224,3584]{1,0:T(8,128)}), f32[1792,3584]{1,0:T(8,128)}) %all-gather.7.cloned.1.call-update) | async-done | bytes 25690128 | tf_op jit(solution)/shard_map/all_gather | solution.py:43
  599.5 11.5 %reduce_sum.39 = f32[224,3584]{1,0:T(8,128)} reduce(f32[8,224,3584]{2,1,0:T(8,128)} %bitcast.30, f32[]{:T(128)} %constant.6.clone.1), dimensions={0}, to_apply=%region_2.3 | reduce | flops 5619712 | bytes 28901380 | tf_op jit(solution)/shard_map/reduce_sum | solution.py:43
  611.1 2.9 fusion.3
  614.0 1.1 copy-done.2
  615.1 1.3 fusion.5
  616.5 3.4 fusion
  619.9 2.6 psum.23
  622.5 12.2 %all-reduce.5.cloned.1.call-done = f32[224,256]{1,0:T(8,128)} async-done(((f32[224,256]{1,0:T(8,128)}), f32[224,256]{1,0:T(8,128)}) %all-reduce.5.cloned.1.call-update) | async-done | bytes 229392 | tf_op jit(solution)/shard_map/psum | solution.py:49
  634.7 1.0 multiply_convert_fusion
  635.7 6.0 all_gather.15
  641.7 2.1 fusion.4
  643.8 1.5 reduce_sum.41
  645.3 2.2 copy.10
  647.5 20.1 %reduce-scatter.5.cloned.1.call-done = bf16[1792,256]{1,0:T(8,128)(2,1)} async-done(((bf16[3584,256]{1,0:T(8,128)(2,1)}), bf16[1792,256]{1,0:T(8,128)(2,1)}) %reduce-scatter.5.cloned.1.call-update) | async-done | bytes 917520 | tf_op jit(solution)/shard_map/reduce_scatter | solution.py:57
  (31 shorter events, 2.4 us)
Async XLA Ops:
  7.2 28.7 %copy-start = (bf16[1,1792,256]{2,1,0:T(8,128)(2,1)S(1)}, bf16[1,1792,256]{2,1,0:T(8,128)(2,1)}, u32[]{:S(2)}) copy-start(bf16[1,1792,256]{2,1,0:T(8,128)(2,1)} %param.8) | copy-start | bytes 2752516
  7.2 44.7 %reduce-scatter.3.cloned.1.call-start = ((), (), s32[]{:S(2)}) async-start(), calls=%async_computation.3 | async-start | bytes 688128 | tf_op jit(solution)/shard_map/reduce_scatter | solution.py:31
  34.7 1.2 copy-start.3
  35.9 16.7 %copy-start.7 = (s32[224]{0:T(256)S(1)}, s32[224]{0:T(256)}, u32[]{:S(2)}) copy-start(s32[224]{0:T(256)} %param.7) | copy-start | bytes 2692
  35.9 36.4 %copy-start.6 = (f32[256]{0:T(256)S(1)}, f32[256]{0:T(256)}, u32[]{:S(2)}) copy-start(f32[256]{0:T(256)} %param.9) | copy-start | bytes 3076
  37.3 35.0 %all-reduce.3.cloned.1.call-start = ((), (), s32[]{:S(2)}) async-start(), calls=%async_computation.4 | async-start | bytes 458752 | tf_op jit(solution)/shard_map/psum | solution.py:37
  51.9 53.4 %all-gather.5.cloned.1.call-start = ((), (), s32[]{:S(2)}) async-start(), calls=%async_computation.7 | async-start | bytes 2752512 | tf_op jit(solution)/shard_map/all_gather | solution.py:39
  52.6 546.9 %all-gather.7.cloned.1.call-start = ((), (), s32[]{:S(2)}) async-start(), calls=%async_computation.8 | async-start | bytes 28901376 | tf_op jit(solution)/shard_map/all_gather | solution.py:43
  109.2 0.7 copy-start.5
  109.2 1.5 copy-start.1
  109.2 525.5 %all-reduce.5.cloned.1.call-start = ((), (), s32[]{:S(2)}) async-start(), calls=%async_computation.5 | async-start | bytes 458752 | tf_op jit(solution)/shard_map/psum | solution.py:49
  614.0 1.2 copy-start.2
  616.4 51.2 %reduce-scatter.5.cloned.1.call-start = ((), (), s32[]{:S(2)}) async-start(), calls=%async_computation.6 | async-start | bytes 2752512 | tf_op jit(solution)/shard_map/reduce_scatter | solution.py:57
  619.8 14.8 %copy-start.4 = (f32[224,256]{1,0:T(8,128)S(1)}, f32[224,256]{1,0:T(8,128)}, u32[]{:S(2)}) copy-start(f32[224,256]{1,0:T(8,128)} %all-reduce.3.cloned.1.call-done) | copy-start | bytes 688132
Sparse Core Ops, SparseCore 0:
  37.4 14.3 reduce-scatter.2
  54.2 18.1 all-reduce.2
  73.9 31.3 all-gather.4
  109.3 490.1 all-gather.6
  616.5 18.0 all-reduce.4
  637.3 30.2 reduce-scatter.4
